TPU v7x, 32 devices: a whole 2x2x4 slice. The times are simulated.
32 devices in a mesh: pos: 8 (over y, x, core), ang: 4 (over z).
Axes of the slice: x: 2, y: 2, z: 4, core: 2. Of those that a mesh axis runs over, the one named last changes fastest.
Arguments:
- object_field: float32 [2, 32, 256, 256], P(None, None, 'pos'), may hold values from -2.5 to 2.5
- probe_wave: float32 [2, 128, 128], replicated, may hold values from -4 to 4
- intensity: float32 [4, 32, 128, 128], P('ang', 'pos'), may hold values from 0.25 to 4
- positions: int32 [32, 2], P('pos'), may hold values from 0 to 255, as said below
- shear_steps: int32 [4, 32], replicated, may hold values from -8 to 8, as said below
Outputs:
- object_new: float32 [2, 32, 256, 256], P(None, None, 'pos')
Inputs may be any that keep to these rules, and one draw needn't show every extreme that they name: `positions`: row j is (column offset, row offset). With d = j // 4 and q = j mod 4: (column offset - d * 32 + 128 // 2) mod 256 lies in 0 .. 32; it is 0 for q = 0 and 32 for q = 1; the row offset lies in 0 .. 128, and is 128 for q = 0 and 0 for q = 1. For every angle a, shear_steps[a, 0] = -8 and shear_steps[a, 31] = 8.
All inputs are finite; a program needn't handle non-finite values.
Results may differ from a plain program's by a relative error of at most 0.0001.
Values sent between devices are 32-bit elements; how exact they have to be, the bound alone decides.
A program may use at most 64 MiB of HBM per device.

v0:
```python
import math
import jax
import jax.numpy as jnp
from jax import lax
from jax.sharding import PartitionSpec as P

FRAME = 128
Y = 256
SH = 8
ITERS = 3
MODULUS_FLOOR = 0.25
INTERSECTION_WEIGHT = 1.0
RELAXATION = 0.5
HIGHEST = lax.Precision.HIGHEST


def padded_2(block, sides, width):
    for axis, dim in sides:
        count = lax.axis_size(axis)
        forward = [(i, i + 1) for i in range(count - 1)]
        forward.append((count - 1, 0))
        backward = [(target, source) for source, target in forward]
        low = lax.ppermute(
            lax.slice_in_dim(block, block.shape[dim] - width, None, axis=dim), axis, forward
        )
        high = lax.ppermute(lax.slice_in_dim(block, 0, width, axis=dim), axis, backward)
        block = jnp.concatenate([low, block, high], axis=dim)
    return block


def passed_along(value, axis, steps):
    count = lax.axis_size(axis)
    pairs = [(source, (source + steps) % count) for source in range(count)]
    return lax.ppermute(value, axis, pairs)


def fourier_tables(length):
    indices = jnp.arange(length, dtype=jnp.int32)
    phases = (indices[:, None] * indices[None, :] % length).astype(jnp.float32) * (
        2.0 * math.pi / length
    )
    factor = 1.0 / math.sqrt(length)
    return (jnp.cos(phases) * factor, jnp.sin(phases) * factor)


def transform(real_part, imag_part, cosine, sine_table, exponent_sign):
    left_real = jnp.einsum(
        "jk,abkl->abjl", cosine, real_part, precision=HIGHEST
    ) - exponent_sign * jnp.einsum("jk,abkl->abjl", sine_table, imag_part, precision=HIGHEST)
    left_imag = jnp.einsum(
        "jk,abkl->abjl", cosine, imag_part, precision=HIGHEST
    ) + exponent_sign * jnp.einsum("jk,abkl->abjl", sine_table, real_part, precision=HIGHEST)
    out_real = jnp.einsum(
        "abjk,kl->abjl", left_real, cosine, precision=HIGHEST
    ) - exponent_sign * jnp.einsum("abjk,kl->abjl", left_imag, sine_table, precision=HIGHEST)
    out_imag = jnp.einsum(
        "abjk,kl->abjl", left_imag, cosine, precision=HIGHEST
    ) + exponent_sign * jnp.einsum("abjk,kl->abjl", left_real, sine_table, precision=HIGHEST)
    return (out_real, out_imag)


def deposit(target, get_piece, start_cols, start_rows, frame_total):
    leading = target.ndim - 2

    def add_one(frame_index, running):
        corner = (0,) * leading + (start_cols[frame_index], start_rows[frame_index])
        addition = get_piece(frame_index)
        current = lax.dynamic_slice(running, corner, addition.shape)
        return lax.dynamic_update_slice(running, current + addition, corner)

    return lax.fori_loop(0, frame_total, add_one, target)


def extract(source, start_cols, start_rows):
    leading = source.shape[:-2]

    def window_at(col_start, row_start):
        return lax.dynamic_slice(
            source, (0,) * len(leading) + (col_start, row_start), leading + (FRAME, FRAME)
        )

    return jax.vmap(window_at, out_axes=2)(start_cols, start_rows)


def per_device(object_field, probe_wave, intensity, positions, shear_steps):
    tile_width = object_field.shape[2]
    full_width = tile_width * lax.axis_size("pos")
    pos_index = lax.axis_index("pos")
    angle_count = intensity.shape[0]
    frame_total = positions.shape[0]
    angle_first = lax.axis_index("ang") * angle_count
    reach_tiles = -(-(FRAME // 2) // tile_width)
    band_count = 2 * reach_tiles + 1
    padded_width = tile_width + 2 * SH
    columns = jnp.arange(tile_width, dtype=jnp.int32)
    padded_cols = jnp.arange(padded_width, dtype=jnp.int32)
    my_steps = lax.dynamic_slice_in_dim(shear_steps, angle_first, angle_count, 0)
    padded = padded_2(object_field, (("pos", 2),), SH)
    forward_pick = (
        padded_cols[None, None, None, :]
        == columns[None, None, :, None] + SH + my_steps[:, :, None, None]
    ).astype(jnp.float32)
    projected = jnp.einsum("azxk,czky->acxy", forward_pick, padded, precision=HIGHEST)
    start_rows = positions[:, 1]
    start_cols = (positions[:, 0] - pos_index * tile_width + reach_tiles * tile_width) % full_width
    work_width = band_count * tile_width
    probe_real = probe_wave[0]
    probe_imag = probe_wave[1]
    probe_power = probe_real * probe_real + probe_imag * probe_imag
    cover_plane = deposit(
        jnp.zeros((work_width, Y), jnp.float32),
        lambda frame_index: probe_power,
        start_cols,
        start_rows,
        frame_total,
    )
    coverage = cover_plane[reach_tiles * tile_width : (reach_tiles + 1) * tile_width]
    for offset in range(band_count):
        if offset != reach_tiles:
            coverage = coverage + passed_along(
                cover_plane[offset * tile_width : (offset + 1) * tile_width],
                "pos",
                offset - reach_tiles,
            )
    cosine, sine_table = fourier_tables(FRAME)
    amplitude = jnp.sqrt(intensity)
    estimate = projected
    for iteration in range(ITERS):
        pieces = []
        for offset in range(band_count):
            if offset == reach_tiles:
                pieces.append(estimate)
            else:
                pieces.append(passed_along(estimate, "pos", reach_tiles - offset))
        source = jnp.concatenate(pieces, axis=2)
        patches = extract(source, start_cols, start_rows)
        patch_real = patches[:, 0]
        patch_imag = patches[:, 1]
        wave_real = probe_real * patch_real - probe_imag * patch_imag
        wave_imag = probe_real * patch_imag + probe_imag * patch_real
        freq_real, freq_imag = transform(wave_real, wave_imag, cosine, sine_table, -1.0)
        modulus = jnp.sqrt(freq_real * freq_real + freq_imag * freq_imag)
        factor = amplitude / jnp.maximum(modulus, MODULUS_FLOOR)
        exit_real, exit_imag = transform(
            freq_real * factor, freq_imag * factor, cosine, sine_table, 1.0
        )
        back_real = probe_real * exit_real + probe_imag * exit_imag
        back_imag = probe_real * exit_imag - probe_imag * exit_real
        contrib = jnp.stack([back_real, back_imag], axis=1)
        summed = deposit(
            jnp.zeros((angle_count, 2, work_width, Y), jnp.float32),
            lambda frame_index: contrib[:, :, frame_index],
            start_cols,
            start_rows,
            frame_total,
        )
        numerator = summed[:, :, reach_tiles * tile_width : (reach_tiles + 1) * tile_width]
        for offset in range(band_count):
            if offset != reach_tiles:
                numerator = numerator + passed_along(
                    summed[:, :, offset * tile_width : (offset + 1) * tile_width],
                    "pos",
                    offset - reach_tiles,
                )
        estimate = (numerator + INTERSECTION_WEIGHT * estimate) / (coverage + INTERSECTION_WEIGHT)
    change = estimate - projected
    change_rim = padded_2(change, (("pos", 2),), SH)
    every_rim = lax.all_gather(change_rim, "ang", axis=0, tiled=True)
    back_pick = (
        padded_cols[None, None, None, :]
        == columns[None, None, :, None] + SH - shear_steps[:, :, None, None]
    ).astype(jnp.float32)
    accumulated = jnp.einsum("azxk,acky->czxy", back_pick, every_rim, precision=HIGHEST)
    return object_field + RELAXATION / shear_steps.shape[0] * accumulated


def solution(mesh):
    placed = (P(None, None, "pos", None), P(), P("ang", "pos", None, None), P("pos", None), P())
    return jax.shard_map(
        per_device,
        mesh=mesh,
        in_specs=placed,
        out_specs=P(None, None, "pos", None),
        check_vma=False,
    )
```

profile of v0, /device:TPU:0, one launch (start us, length us, event | category | flops | bytes accessed | tf_op | source)
XLA Modules:
  0.0 269.1 jit_solution(3598538774012352433)
XLA Ops:
  0.0 2.3 fusion.380
  2.8 2.9 %collective-permute-start.1 = (f32[2,32,8,256]{3,2,1,0:T(8,128)S(1)}, f32[2,32,8,256]{3,2,1,0:T(8,128)}, u32[]{:S(2)}, u32[]{:S(2)}) collective-permute-start(f32[2,32,8,256]{3,2,1,0:T(8,128)S(1)} %get-tuple-element.525), channel_id=1, source_target_pairs={{4,0},{8,4},{12,8},{16,12},{20,16},{24,20},{28,24},{0,28},{5,1},{9... | collective-permute-start | bytes 1572872 | tf_op jit(solution)/shard_map/ppermute | solution.py:26
  6.8 25.6 %while.56 = (s32[]{:T(128)}, f32[160,256]{1,0:T(8,128)S(1)}, s32[4]{0:T(128)S(1)}, s32[4]{0:T(128)S(1)}, f32[128,128]{1,0:T(8,128)S(1)}, /*index=5*/s32[]{:T(128)}, s32[]{:T(128)}, s32[]{:T(128)}, s32[]{:T(128)}) while((s32[]{:T(128)}, f32[160,256]{1,0:T(8,128)S(1)}, s32[4]{0:T(128)S(1)}, s32[4]{0:T(128)S(1)}, f32[128,128]{1,0:T(8,128)S(1)}, ...), condition=%wide.region_3.4_spmd, body=%wide.region_2.3_spmd.sunk | while | flops 16392 | bytes 327877 | solution.py:71
  24.0 1.7 dynamic_update_slice.33
  30.7 1.7 dynamic_update_slice.33
  33.1 2.4 collective-permute-start.10
  36.3 2.5 fusion.35
  38.8 2.0 collective-permute-start.2
  40.9 3.6 %collective-permute-done.2 = f32[1,2,32,256]{3,2,1,0:T(8,128)S(1)} collective-permute-done((f32[1,2,32,256]{3,2,1,0:T(8,128)S(1)}, f32[1,2,32,256]{3,2,1,0:T(8,128)S(1)}, u32[]{:S(2)}, u32[]{:S(2)}) %collective-permute-start.2) | collective-permute-done | bytes 65568 | tf_op jit(solution)/shard_map/ppermute | solution.py:34
  44.6 4.5 %collective-permute-done.3 = f32[1,2,32,256]{3,2,1,0:T(8,128)S(1)} collective-permute-done((f32[1,2,32,256]{3,2,1,0:T(8,128)S(1)}, f32[1,2,32,256]{3,2,1,0:T(8,128)S(1)}, u32[]{:S(2)}, u32[]{:S(2)}) %collective-permute-start.3) | collective-permute-done | bytes 65568 | tf_op jit(solution)/shard_map/ppermute | solution.py:34
  49.1 1.9 collective-permute-done.4
  51.7 3.6 %collective-permute-done.5 = f32[1,2,32,256]{3,2,1,0:T(8,128)S(1)} collective-permute-done((f32[1,2,32,256]{3,2,1,0:T(8,128)S(1)}, f32[1,2,32,256]{3,2,1,0:T(8,128)S(1)}, u32[]{:S(2)}, u32[]{:S(2)}) %collective-permute-start.5) | collective-permute-done | bytes 65568 | tf_op jit(solution)/shard_map/ppermute | solution.py:34
  55.3 8.7 %while.59 = (s32[]{:T(128)}, f32[1,2,160,256]{3,2,1,0:T(8,128)S(1)}, s32[4,4]{1,0:T(4,128)S(1)}, f32[4,1,2,128,128]{4,3,0,2,1:T(8,128)S(1)}, s32[]{:T(128)}) while((s32[]{:T(128)}, f32[1,2,160,256]{3,2,1,0:T(8,128)S(1)}, s32[4,4]{1,0:T(4,128)S(1)}, f32[4,1,2,128,128]{4,3,0,2,1:T(8,128)S(1)}, s32[]{:T(128)}) %tuple.172), condition=%wide.while_cond, body=%wide.while_body.sunk | while | flops 2 | bytes 262269 | solution.py:78
  56.0 1.4 bitcast_dynamic-update-slice_fusion.6
  58.0 1.4 bitcast_dynamic-update-slice_fusion.6
  60.1 1.4 bitcast_dynamic-update-slice_fusion.6
  76.2 29.0 %while.55 = (s32[]{:T(128)}, f32[1,2,160,256]{3,2,1,0:T(8,128)S(1)}, s32[4]{0:T(128)S(1)}, s32[4]{0:T(128)S(1)}, f32[1,2,4,128,128]{4,3,2,1,0:T(8,128)S(1)}, /*index=5*/s32[]{:T(128)}, s32[]{:T(128)}, s32[]{:T(128)}, s32[]{:T(128)}) while((s32[]{:T(128)}, f32[1,2,160,256]{3,2,1,0:T(8,128)S(1)}, s32[4]{0:T(128)S(1)}, s32[4]{0:T(128)S(1)}, ...), condition=%wide.region_1.2_spmd, body=%wide.region_0.1_spmd.sunk | while | flops 32776 | bytes 655561 | solution.py:71
  95.4 2.1 dynamic_update_slice.32
  103.1 2.1 dynamic_update_slice.32
  105.3 1.8 collective-permute-start.6
  110.6 2.3 collective-permute-done.8
  112.9 2.0 collective-permute-done.9
  115.1 2.6 collective-permute-start.16
  117.7 2.0 collective-permute-start.17
  120.4 1.8 collective-permute-done.17
  122.2 7.8 %while.60 = (s32[]{:T(128)}, f32[1,2,160,256]{3,2,1,0:T(8,128)S(1)}, s32[4,4]{1,0:T(4,128)S(1)}, f32[4,1,2,128,128]{4,3,0,2,1:T(8,128)S(1)}, s32[]{:T(128)}) while((s32[]{:T(128)}, f32[1,2,160,256]{3,2,1,0:T(8,128)S(1)}, s32[4,4]{1,0:T(4,128)S(1)}, f32[4,1,2,128,128]{4,3,0,2,1:T(8,128)S(1)}, s32[]{:T(128)}) %tuple.193), condition=%wide.while_cond.1, body=%wide.while_body.1.sunk | while | flops 2 | bytes 262269 | solution.py:78
  142.3 29.0 %while.57 = (s32[]{:T(128)}, f32[1,2,160,256]{3,2,1,0:T(8,128)S(1)}, s32[4]{0:T(128)S(1)}, s32[4]{0:T(128)S(1)}, f32[1,2,4,128,128]{4,3,2,1,0:T(8,128)S(1)}, /*index=5*/s32[]{:T(128)}, s32[]{:T(128)}, s32[]{:T(128)}, s32[]{:T(128)}) while((s32[]{:T(128)}, f32[1,2,160,256]{3,2,1,0:T(8,128)S(1)}, s32[4]{0:T(128)S(1)}, s32[4]{0:T(128)S(1)}, ...), condition=%wide.region_5.6_spmd, body=%wide.region_4.5_spmd.sunk | while | flops 32776 | bytes 655561 | solution.py:71
  161.5 2.1 dynamic_update_slice.34
  169.2 2.1 dynamic_update_slice.34
  171.4 2.8 %collective-permute-start.18 = (f32[1,2,32,256]{3,2,1,0:T(8,128)S(1)}, f32[1,2,32,256]{3,2,1,0:T(8,128)S(1)}, u32[]{:S(2)}, u32[]{:S(2)}) collective-permute-start(f32[1,2,32,256]{3,2,1,0:T(8,128)S(1)} %get-tuple-element.542), channel_id=1, source_target_pairs={{0,24},{4,28},{8,0},{12,4},{16,8},{20,12},{24,16},{28,20},{1,25},{... | collective-permute-start | bytes 196616 | tf_op jit(solution)/shard_map/ppermute | solution.py:34
  174.7 1.8 collective-permute-done.18
  176.5 1.4 collective-permute-done.19
  178.8 1.4 collective-permute-done.21
  181.2 2.6 collective-permute-start.24
  186.2 1.9 collective-permute-done.25
  188.2 8.2 %while.61 = (s32[]{:T(128)}, f32[1,2,160,256]{3,2,1,0:T(8,128)S(1)}, s32[4,4]{1,0:T(4,128)S(1)}, f32[4,1,2,128,128]{4,3,0,2,1:T(8,128)S(1)}, s32[]{:T(128)}) while((s32[]{:T(128)}, f32[1,2,160,256]{3,2,1,0:T(8,128)S(1)}, s32[4,4]{1,0:T(4,128)S(1)}, f32[4,1,2,128,128]{4,3,0,2,1:T(8,128)S(1)}, s32[]{:T(128)}) %tuple.194), condition=%wide.while_cond.2, body=%wide.while_body.2.sunk | while | flops 2 | bytes 262269 | solution.py:78
  188.8 1.4 bitcast_dynamic-update-slice_fusion.8
  190.9 1.4 bitcast_dynamic-update-slice_fusion.8
  208.7 29.0 %while.58 = (s32[]{:T(128)}, f32[1,2,160,256]{3,2,1,0:T(8,128)S(1)}, s32[4]{0:T(128)S(1)}, s32[4]{0:T(128)S(1)}, f32[1,2,4,128,128]{4,3,2,1,0:T(8,128)S(1)}, /*index=5*/s32[]{:T(128)}, s32[]{:T(128)}, s32[]{:T(128)}, s32[]{:T(128)}) while((s32[]{:T(128)}, f32[1,2,160,256]{3,2,1,0:T(8,128)S(1)}, s32[4]{0:T(128)S(1)}, s32[4]{0:T(128)S(1)}, ...), condition=%wide.region_7.8_spmd, body=%wide.region_6.7_spmd.sunk | while | flops 32776 | bytes 655561 | solution.py:71
  227.8 2.1 dynamic_update_slice.35
  235.6 2.1 dynamic_update_slice.35
  237.8 2.2 collective-permute-start.26
  240.5 1.7 collective-permute-done.26
  242.2 1.4 collective-permute-done.27
  244.5 1.4 collective-permute-done.29
  246.0 2.6 collective-permute-start.31
  250.1 15.1 %all_gather.3 = f32[4,2,48,256]{3,2,1,0:T(8,128)S(1)} all-gather(f32[1,2,48,256]{3,2,1,0:T(8,128)S(1)} %pad_maximum_fusion.3), channel_id=1, replica_groups=mesh['pos'=8,'ang'=4] {'ang'}, dimensions={0}, use_global_device_ids=true | all-gather | bytes 491520 | tf_op jit(solution)/shard_map/all_gather | solution.py:168
  265.2 3.6 %bitcast_add_fusion.3 = f32[2,32,32,256]{3,2,1,0:T(8,128)} fusion(f32[2,32,32,256]{3,2,1,0:T(8,128)S(1)} %copy-done, s32[4,32,32]{2,0,1:T(4,128)S(1)} %broadcast_subtract_fusion, f32[4,2,48,256]{3,2,1,0:T(8,128)S(1)} %all_gather.3), kind=kOutput, calls=%fused_computation.16 | convolution fusion | flops 1209204736 | bytes 4603904 | tf_op jit(solution)/shard_map/azxk,acky->czxy/dot_general | solution.py:173
  (244 shorter events, 101.2 us)
Async XLA Ops:
  0.0 36.3 %copy-start = (f32[2,32,32,256]{3,2,1,0:T(8,128)S(1)}, f32[2,32,32,256]{3,2,1,0:T(8,128)}, u32[]{:S(2)}) copy-start(f32[2,32,32,256]{3,2,1,0:T(8,128)} %param.13) | copy-start | bytes 6291460
  0.0 5.6 %copy-start.3 = (s32[4,2]{0,1:T(2,128)S(1)}, s32[4,2]{0,1:T(2,128)}, u32[]{:S(2)}) copy-start(s32[4,2]{0,1:T(2,128)} %param.16) | copy-start | bytes 100
  0.0 36.2 %copy-start.1 = (f32[2,128,128]{2,1,0:T(8,128)S(1)}, f32[2,128,128]{2,1,0:T(8,128)}, u32[]{:S(2)}) copy-start(f32[2,128,128]{2,1,0:T(8,128)} %param.14) | copy-start | bytes 393220
  0.0 36.1 %copy-start.2 = (s32[4,32]{1,0:T(4,128)S(1)}, s32[4,32]{1,0:T(4,128)}, u32[]{:S(2)}) copy-start(s32[4,32]{1,0:T(4,128)} %param.17) | copy-start | bytes 1540
  2.3 33.9 %collective-permute-start = (f32[2,32,8,256]{3,2,1,0:T(8,128)}, f32[2,32,8,256]{3,2,1,0:T(8,128)}, u32[]{:S(2)}, u32[]{:S(2)}) collective-permute-start(f32[2,32,8,256]{3,2,1,0:T(8,128)} %get-tuple-element.524), channel_id=1, source_target_pairs={{0,4},{4,8},{8,12},{12,16},{16,20},{20,24},{24,28},{28,0},{1,5},{5... | collective-permute-start | bytes 1572872 | tf_op jit(solution)/shard_map/ppermute | solution.py:23
  2.8 33.5 %collective-permute-start.1 = (f32[2,32,8,256]{3,2,1,0:T(8,128)S(1)}, f32[2,32,8,256]{3,2,1,0:T(8,128)}, u32[]{:S(2)}, u32[]{:S(2)}) collective-permute-start(f32[2,32,8,256]{3,2,1,0:T(8,128)S(1)} %get-tuple-element.525), channel_id=1, source_target_pairs={{4,0},{8,4},{12,8},{16,12},{20,16},{24,20},{28,24},{0,28},{5,1},{9... | collective-permute-start | bytes 1572872 | tf_op jit(solution)/shard_map/ppermute | solution.py:26
  33.1 74.0 %collective-permute-start.10 = (f32[32,256]{1,0:T(8,128)}, f32[32,256]{1,0:T(8,128)S(1)}, u32[]{:S(2)}, u32[]{:S(2)}) collective-permute-start(f32[32,256]{1,0:T(8,128)} %get-tuple-element.550), channel_id=1, source_target_pairs={{0,24},{4,28},{8,0},{12,4},{16,8},{20,12},{24,16},{28,20},{1,25},{... | collective-permute-start | bytes 98312 | tf_op jit(solution)/shard_map/ppermute | solution.py:34
  35.5 72.8 %collective-permute-start.11 = (f32[32,256]{1,0:T(8,128)}, f32[32,256]{1,0:T(8,128)S(1)}, u32[]{:S(2)}, u32[]{:S(2)}) collective-permute-start(f32[32,256]{1,0:T(8,128)} %get-tuple-element.553), channel_id=1, source_target_pairs={{0,28},{4,0},{8,4},{12,8},{16,12},{20,16},{24,20},{28,24},{1,29},{... | collective-permute-start | bytes 98312 | tf_op jit(solution)/shard_map/ppermute | solution.py:34
  35.5 72.8 %collective-permute-start.12 = (f32[32,256]{1,0:T(8,128)}, f32[32,256]{1,0:T(8,128)}, u32[]{:S(2)}, u32[]{:S(2)}) collective-permute-start(f32[32,256]{1,0:T(8,128)} %get-tuple-element.552), channel_id=1, source_target_pairs={{0,4},{4,8},{8,12},{12,16},{16,20},{20,24},{24,28},{28,0},{1,5},{5... | collective-permute-start | bytes 98312 | tf_op jit(solution)/shard_map/ppermute | solution.py:34
  36.2 73.3 %collective-permute-start.13 = (f32[32,256]{1,0:T(8,128)}, f32[32,256]{1,0:T(8,128)}, u32[]{:S(2)}, u32[]{:S(2)}) collective-permute-start(f32[32,256]{1,0:T(8,128)} %get-tuple-element.551), channel_id=1, source_target_pairs={{0,8},{4,12},{8,16},{12,20},{16,24},{20,28},{24,0},{28,4},{1,9},{5... | collective-permute-start | bytes 98312 | tf_op jit(solution)/shard_map/ppermute | solution.py:34
  38.8 5.6 %collective-permute-start.2 = (f32[1,2,32,256]{3,2,1,0:T(8,128)S(1)}, f32[1,2,32,256]{3,2,1,0:T(8,128)S(1)}, u32[]{:S(2)}, u32[]{:S(2)}) collective-permute-start(f32[1,2,32,256]{3,2,1,0:T(8,128)S(1)} %fusion.35), channel_id=1, source_target_pairs={{0,8},{4,12},{8,16},{12,20},{16,24},{20,28},{24,0},{28,4},{1,9},{5... | collective-permute-start | bytes 196616 | tf_op jit(solution)/shard_map/ppermute | solution.py:34
  44.5 4.6 %collective-permute-start.3 = (f32[1,2,32,256]{3,2,1,0:T(8,128)S(1)}, f32[1,2,32,256]{3,2,1,0:T(8,128)S(1)}, u32[]{:S(2)}, u32[]{:S(2)}) collective-permute-start(f32[1,2,32,256]{3,2,1,0:T(8,128)S(1)} %fusion.35), channel_id=1, source_target_pairs={{0,4},{4,8},{8,12},{12,16},{16,20},{20,24},{24,28},{28,0},{1,5},{5... | collective-permute-start | bytes 196616 | tf_op jit(solution)/shard_map/ppermute | solution.py:34
  49.0 1.9 collective-permute-start.4
  51.0 4.3 %collective-permute-start.5 = (f32[1,2,32,256]{3,2,1,0:T(8,128)S(1)}, f32[1,2,32,256]{3,2,1,0:T(8,128)S(1)}, u32[]{:S(2)}, u32[]{:S(2)}) collective-permute-start(f32[1,2,32,256]{3,2,1,0:T(8,128)S(1)} %fusion.35), channel_id=1, source_target_pairs={{0,24},{4,28},{8,0},{12,4},{16,8},{20,12},{24,16},{28,20},{1,25},{... | collective-permute-start | bytes 196616 | tf_op jit(solution)/shard_map/ppermute | solution.py:34
  64.8 4.5 %copy-start.4 = (f32[1,4,128,128]{3,2,1,0:T(8,128)S(1)}, f32[1,4,128,128]{3,2,1,0:T(8,128)}, u32[]{:S(2)}) copy-start(f32[1,4,128,128]{3,2,1,0:T(8,128)} %param.15) | copy-start | bytes 786436
  105.3 4.2 %copy-start.7 = (s32[4]{0:T(128)}, s32[4]{0:T(128)S(1)}, u32[]{:S(2)}) copy-start(s32[4]{0:T(128)S(1)} %get-tuple-element.988) | copy-start | bytes 52
  105.3 5.0 %collective-permute-start.6 = (f32[1,2,32,256]{3,2,1,0:T(8,128)S(1)}, f32[1,2,32,256]{3,2,1,0:T(8,128)S(1)}, u32[]{:S(2)}, u32[]{:S(2)}) collective-permute-start(f32[1,2,32,256]{3,2,1,0:T(8,128)S(1)} %get-tuple-element.546), channel_id=1, source_target_pairs={{0,24},{4,28},{8,0},{12,4},{16,8},{20,12},{24,16},{28,20},{1,25},{... | collective-permute-start | bytes 196616 | tf_op jit(solution)/shard_map/ppermute | solution.py:34
  107.1 3.5 %collective-permute-start.7 = (f32[1,2,32,256]{3,2,1,0:T(8,128)S(1)}, f32[1,2,32,256]{3,2,1,0:T(8,128)S(1)}, u32[]{:S(2)}, u32[]{:S(2)}) collective-permute-start(f32[1,2,32,256]{3,2,1,0:T(8,128)S(1)} %get-tuple-element.549), channel_id=1, source_target_pairs={{0,28},{4,0},{8,4},{12,8},{16,12},{20,16},{24,20},{28,24},{1,29},{... | collective-permute-start | bytes 196616 | tf_op jit(solution)/shard_map/ppermute | solution.py:34
  108.2 4.7 %collective-permute-start.8 = (f32[1,2,32,256]{3,2,1,0:T(8,128)S(1)}, f32[1,2,32,256]{3,2,1,0:T(8,128)S(1)}, u32[]{:S(2)}, u32[]{:S(2)}) collective-permute-start(f32[1,2,32,256]{3,2,1,0:T(8,128)S(1)} %get-tuple-element.548), channel_id=1, source_target_pairs={{0,4},{4,8},{8,12},{12,16},{16,20},{20,24},{24,28},{28,0},{1,5},{5... | collective-permute-start | bytes 196616 | tf_op jit(solution)/shard_map/ppermute | solution.py:34
  108.2 6.7 %collective-permute-start.9 = (f32[1,2,32,256]{3,2,1,0:T(8,128)S(1)}, f32[1,2,32,256]{3,2,1,0:T(8,128)S(1)}, u32[]{:S(2)}, u32[]{:S(2)}) collective-permute-start(f32[1,2,32,256]{3,2,1,0:T(8,128)S(1)} %get-tuple-element.547), channel_id=1, source_target_pairs={{0,8},{4,12},{8,16},{12,20},{16,24},{20,28},{24,0},{28,4},{1,9},{5... | collective-permute-start | bytes 196616 | tf_op jit(solution)/shard_map/ppermute | solution.py:34
  115.0 5.4 %collective-permute-start.14 = (f32[1,2,32,256]{3,2,1,0:T(8,128)S(1)}, f32[1,2,32,256]{3,2,1,0:T(8,128)S(1)}, u32[]{:S(2)}, u32[]{:S(2)}) collective-permute-start(f32[1,2,32,256]{3,2,1,0:T(8,128)S(1)} %add_divide_fusion.1), channel_id=1, source_target_pairs={{0,8},{4,12},{8,16},{12,20},{16,24},{20,28},{24,0},{28,4},{1,9},{5... | collective-permute-start | bytes 196616 | tf_op jit(solution)/shard_map/ppermute | solution.py:34
  115.0 5.4 %collective-permute-start.15 = (f32[1,2,32,256]{3,2,1,0:T(8,128)S(1)}, f32[1,2,32,256]{3,2,1,0:T(8,128)S(1)}, u32[]{:S(2)}, u32[]{:S(2)}) collective-permute-start(f32[1,2,32,256]{3,2,1,0:T(8,128)S(1)} %add_divide_fusion.1), channel_id=1, source_target_pairs={{0,4},{4,8},{8,12},{12,16},{16,20},{20,24},{24,28},{28,0},{1,5},{5... | collective-permute-start | bytes 196616 | tf_op jit(solution)/shard_map/ppermute | solution.py:34
  115.1 5.3 %collective-permute-start.16 = (f32[1,2,32,256]{3,2,1,0:T(8,128)S(1)}, f32[1,2,32,256]{3,2,1,0:T(8,128)S(1)}, u32[]{:S(2)}, u32[]{:S(2)}) collective-permute-start(f32[1,2,32,256]{3,2,1,0:T(8,128)S(1)} %add_divide_fusion.1), channel_id=1, source_target_pairs={{0,28},{4,0},{8,4},{12,8},{16,12},{20,16},{24,20},{28,24},{1,29},{... | collective-permute-start | bytes 196616 | tf_op jit(solution)/shard_map/ppermute | solution.py:34
  117.7 4.5 %collective-permute-start.17 = (f32[1,2,32,256]{3,2,1,0:T(8,128)S(1)}, f32[1,2,32,256]{3,2,1,0:T(8,128)S(1)}, u32[]{:S(2)}, u32[]{:S(2)}) collective-permute-start(f32[1,2,32,256]{3,2,1,0:T(8,128)S(1)} %add_divide_fusion.1), channel_id=1, source_target_pairs={{0,24},{4,28},{8,0},{12,4},{16,8},{20,12},{24,16},{28,20},{1,25},{... | collective-permute-start | bytes 196616 | tf_op jit(solution)/shard_map/ppermute | solution.py:34
  130.8 4.5 %copy-start.5 = (f32[1,4,128,128]{3,2,1,0:T(8,128)S(1)}, f32[1,4,128,128]{3,2,1,0:T(8,128)}, u32[]{:S(2)}) copy-start(f32[1,4,128,128]{3,2,1,0:T(8,128)} %param.15) | copy-start | bytes 786436
  139.8 2.5 copy-start.8
  171.4 5.1 %collective-permute-start.18 = (f32[1,2,32,256]{3,2,1,0:T(8,128)S(1)}, f32[1,2,32,256]{3,2,1,0:T(8,128)S(1)}, u32[]{:S(2)}, u32[]{:S(2)}) collective-permute-start(f32[1,2,32,256]{3,2,1,0:T(8,128)S(1)} %get-tuple-element.542), channel_id=1, source_target_pairs={{0,24},{4,28},{8,0},{12,4},{16,8},{20,12},{24,16},{28,20},{1,25},{... | collective-permute-start | bytes 196616 | tf_op jit(solution)/shard_map/ppermute | solution.py:34
  174.2 3.7 %collective-permute-start.19 = (f32[1,2,32,256]{3,2,1,0:T(8,128)S(1)}, f32[1,2,32,256]{3,2,1,0:T(8,128)S(1)}, u32[]{:S(2)}, u32[]{:S(2)}) collective-permute-start(f32[1,2,32,256]{3,2,1,0:T(8,128)S(1)} %get-tuple-element.545), channel_id=1, source_target_pairs={{0,28},{4,0},{8,4},{12,8},{16,12},{20,16},{24,20},{28,24},{1,29},{... | collective-permute-start | bytes 196616 | tf_op jit(solution)/shard_map/ppermute | solution.py:34
  174.2 4.6 %collective-permute-start.20 = (f32[1,2,32,256]{3,2,1,0:T(8,128)S(1)}, f32[1,2,32,256]{3,2,1,0:T(8,128)S(1)}, u32[]{:S(2)}, u32[]{:S(2)}) collective-permute-start(f32[1,2,32,256]{3,2,1,0:T(8,128)S(1)} %get-tuple-element.544), channel_id=1, source_target_pairs={{0,4},{4,8},{8,12},{12,16},{16,20},{20,24},{24,28},{28,0},{1,5},{5... | collective-permute-start | bytes 196616 | tf_op jit(solution)/shard_map/ppermute | solution.py:34
  174.7 5.5 %collective-permute-start.21 = (f32[1,2,32,256]{3,2,1,0:T(8,128)S(1)}, f32[1,2,32,256]{3,2,1,0:T(8,128)S(1)}, u32[]{:S(2)}, u32[]{:S(2)}) collective-permute-start(f32[1,2,32,256]{3,2,1,0:T(8,128)S(1)} %get-tuple-element.543), channel_id=1, source_target_pairs={{0,8},{4,12},{8,16},{12,20},{16,24},{20,28},{24,0},{28,4},{1,9},{5... | collective-permute-start | bytes 196616 | tf_op jit(solution)/shard_map/ppermute | solution.py:34
  180.2 5.6 %collective-permute-start.22 = (f32[1,2,32,256]{3,2,1,0:T(8,128)S(1)}, f32[1,2,32,256]{3,2,1,0:T(8,128)S(1)}, u32[]{:S(2)}, u32[]{:S(2)}) collective-permute-start(f32[1,2,32,256]{3,2,1,0:T(8,128)S(1)} %add_divide_fusion), channel_id=1, source_target_pairs={{0,8},{4,12},{8,16},{12,20},{16,24},{20,28},{24,0},{28,4},{1,9},{5... | collective-permute-start | bytes 196616 | tf_op jit(solution)/shard_map/ppermute | solution.py:34
  181.2 5.0 %collective-permute-start.23 = (f32[1,2,32,256]{3,2,1,0:T(8,128)S(1)}, f32[1,2,32,256]{3,2,1,0:T(8,128)S(1)}, u32[]{:S(2)}, u32[]{:S(2)}) collective-permute-start(f32[1,2,32,256]{3,2,1,0:T(8,128)S(1)} %add_divide_fusion), channel_id=1, source_target_pairs={{0,4},{4,8},{8,12},{12,16},{16,20},{20,24},{24,28},{28,0},{1,5},{5... | collective-permute-start | bytes 196616 | tf_op jit(solution)/shard_map/ppermute | solution.py:34
  181.2 5.0 %collective-permute-start.24 = (f32[1,2,32,256]{3,2,1,0:T(8,128)S(1)}, f32[1,2,32,256]{3,2,1,0:T(8,128)S(1)}, u32[]{:S(2)}, u32[]{:S(2)}) collective-permute-start(f32[1,2,32,256]{3,2,1,0:T(8,128)S(1)} %add_divide_fusion), channel_id=1, source_target_pairs={{0,28},{4,0},{8,4},{12,8},{16,12},{20,16},{24,20},{28,24},{1,29},{... | collective-permute-start | bytes 196616 | tf_op jit(solution)/shard_map/ppermute | solution.py:34
  183.8 4.3 %collective-permute-start.25 = (f32[1,2,32,256]{3,2,1,0:T(8,128)S(1)}, f32[1,2,32,256]{3,2,1,0:T(8,128)S(1)}, u32[]{:S(2)}, u32[]{:S(2)}) collective-permute-start(f32[1,2,32,256]{3,2,1,0:T(8,128)S(1)} %add_divide_fusion), channel_id=1, source_target_pairs={{0,24},{4,28},{8,0},{12,4},{16,8},{20,12},{24,16},{28,20},{1,25},{... | collective-permute-start | bytes 196616 | tf_op jit(solution)/shard_map/ppermute | solution.py:34
  197.1 4.5 %copy-start.6 = (f32[1,4,128,128]{3,2,1,0:T(8,128)S(1)}, f32[1,4,128,128]{3,2,1,0:T(8,128)}, u32[]{:S(2)}) copy-start(f32[1,4,128,128]{3,2,1,0:T(8,128)} %param.15) | copy-start | bytes 786436
  237.8 4.5 %collective-permute-start.26 = (f32[1,2,32,256]{3,2,1,0:T(8,128)S(1)}, f32[1,2,32,256]{3,2,1,0:T(8,128)S(1)}, u32[]{:S(2)}, u32[]{:S(2)}) collective-permute-start(f32[1,2,32,256]{3,2,1,0:T(8,128)S(1)} %get-tuple-element.538), channel_id=1, source_target_pairs={{0,24},{4,28},{8,0},{12,4},{16,8},{20,12},{24,16},{28,20},{1,25},{... | collective-permute-start | bytes 196616 | tf_op jit(solution)/shard_map/ppermute | solution.py:34
  239.9 3.7 %collective-permute-start.27 = (f32[1,2,32,256]{3,2,1,0:T(8,128)S(1)}, f32[1,2,32,256]{3,2,1,0:T(8,128)S(1)}, u32[]{:S(2)}, u32[]{:S(2)}) collective-permute-start(f32[1,2,32,256]{3,2,1,0:T(8,128)S(1)} %get-tuple-element.541), channel_id=1, source_target_pairs={{0,28},{4,0},{8,4},{12,8},{16,12},{20,16},{24,20},{28,24},{1,29},{... | collective-permute-start | bytes 196616 | tf_op jit(solution)/shard_map/ppermute | solution.py:34
  239.9 4.6 %collective-permute-start.28 = (f32[1,2,32,256]{3,2,1,0:T(8,128)S(1)}, f32[1,2,32,256]{3,2,1,0:T(8,128)S(1)}, u32[]{:S(2)}, u32[]{:S(2)}) collective-permute-start(f32[1,2,32,256]{3,2,1,0:T(8,128)S(1)} %get-tuple-element.540), channel_id=1, source_target_pairs={{0,4},{4,8},{8,12},{12,16},{16,20},{20,24},{24,28},{28,0},{1,5},{5... | collective-permute-start | bytes 196616 | tf_op jit(solution)/shard_map/ppermute | solution.py:34
  240.4 5.5 %collective-permute-start.29 = (f32[1,2,32,256]{3,2,1,0:T(8,128)S(1)}, f32[1,2,32,256]{3,2,1,0:T(8,128)S(1)}, u32[]{:S(2)}, u32[]{:S(2)}) collective-permute-start(f32[1,2,32,256]{3,2,1,0:T(8,128)S(1)} %get-tuple-element.539), channel_id=1, source_target_pairs={{0,8},{4,12},{8,16},{12,20},{16,24},{20,28},{24,0},{28,4},{1,9},{5... | collective-permute-start | bytes 196616 | tf_op jit(solution)/shard_map/ppermute | solution.py:34
  246.0 4.1 %collective-permute-start.30 = (f32[1,2,8,256]{3,2,1,0:T(8,128)S(1)}, f32[1,2,8,256]{3,2,1,0:T(8,128)S(1)}, u32[]{:S(2)}, u32[]{:S(2)}) collective-permute-start(f32[1,2,8,256]{3,2,1,0:T(8,128)S(1)} %get-tuple-element.556), channel_id=1, source_target_pairs={{0,4},{4,8},{8,12},{12,16},{16,20},{20,24},{24,28},{28,0},{1,5},{5... | collective-permute-start | bytes 49160 | tf_op jit(solution)/shard_map/ppermute | solution.py:23
  246.0 4.1 %collective-permute-start.31 = (f32[1,2,8,256]{3,2,1,0:T(8,128)S(1)}, f32[1,2,8,256]{3,2,1,0:T(8,128)S(1)}, u32[]{:S(2)}, u32[]{:S(2)}) collective-permute-start(f32[1,2,8,256]{3,2,1,0:T(8,128)S(1)} %get-tuple-element.557), channel_id=1, source_target_pairs={{4,0},{8,4},{12,8},{16,12},{20,16},{24,20},{28,24},{0,28},{5,1},{9... | collective-permute-start | bytes 49160 | tf_op jit(solution)/shard_map/ppermute | solution.py:26
where the time goes:
time: 273 us; the launch traced here: 269 us
  local copies, waits for them, and re-layouts  73.2 us (27%)
  loops' own time  66.1 us (24%)
  matrix products  42.3 us (15%)
  waiting for transfers between devices  35.9 us (13%)
  starting transfers between devices  31.4 us (12%)
  blocking collectives  15.1 us (6%)
  other arithmetic  4.05 us (1%)
    another operation x4, loops' own time, deposit(): return lax.fori_loop(0, frame_total, add_one, target)  65.2 us
    ppermute x28, waiting for transfers between devices, passed_along(): return lax.ppermute(value, axis, pairs)  34.5 us
    ppermute x28, starting transfers between devices, passed_along(): return lax.ppermute(value, axis, pairs)  25.4 us
    dynamic_update_slice x16, local copies, waits for them, and re-layouts, add_one(): return lax.dynamic_update_slice(running, current + addition, corner)  25 us
    gather x36, local copies, waits for them, and re-layouts  23.8 us
    dynamic_slice x32, local copies, waits for them, and re-layouts, add_one(): corner = (0,) * leading + (start_cols[frame_index], start_rows[frame_index])  20.8 us
    all_gather x1, blocking collectives, per_device(): every_rim = lax.all_gather(change_rim, 'ang', axis=0, tiled=True)  15.1 us
    ppermute x2, starting transfers between devices, padded_2(): lax.ppermute(lax.slice_in_dim(block, 0, width, axis=dim), axis, backward)  5.5 us
  transfers between devices with their start and end apart: 32, of which 21 were waited for; matrix products, arithmetic and copies ran while one was open for 18% of the time, Pallas kernels for 0%

commit v1 on v0

--- a/solution.py
+++ b/solution.py
@@ -165,12 +165,41 @@
         estimate = (numerator + INTERSECTION_WEIGHT * estimate) / (coverage + INTERSECTION_WEIGHT)
     change = estimate - projected
     change_rim = padded_2(change, (("pos", 2),), SH)
-    every_rim = lax.all_gather(change_rim, "ang", axis=0, tiled=True)
     back_pick = (
         padded_cols[None, None, None, :]
         == columns[None, None, :, None] + SH - shear_steps[:, :, None, None]
     ).astype(jnp.float32)
-    accumulated = jnp.einsum("azxk,acky->czxy", back_pick, every_rim, precision=HIGHEST)
+    size, place, rows = (lax.axis_size("ang"), lax.axis_index("ang"), change_rim.shape[0])
+    right = [(i_2, (i_2 + 1) % size) for i_2 in range(size)]
+    backward_2 = [(i_2, (i_2 - 1) % size) for i_2 in range(size)]
+    half = size // 2
+    from_left = from_right = change_rim
+    accumulated = jnp.einsum(
+        "azxk,acky->czxy",
+        lax.dynamic_slice_in_dim(back_pick, place * rows, change_rim.shape[0], axis=0),
+        change_rim,
+        precision=HIGHEST,
+    )
+    for step in range(1, half + 1):
+        from_left = lax.ppermute(from_left, "ang", right)
+        if step < size - half:
+            from_right = lax.ppermute(from_right, "ang", backward_2)
+            accumulated = accumulated + jnp.einsum(
+                "azxk,acky->czxy",
+                lax.dynamic_slice_in_dim(
+                    back_pick, (place + step) % size * rows, from_right.shape[0], axis=0
+                ),
+                from_right,
+                precision=HIGHEST,
+            )
+        accumulated = accumulated + jnp.einsum(
+            "azxk,acky->czxy",
+            lax.dynamic_slice_in_dim(
+                back_pick, (place - step) % size * rows, from_left.shape[0], axis=0
+            ),
+            from_left,
+            precision=HIGHEST,
+        )
     return object_field + RELAXATION / shear_steps.shape[0] * accumulated
 
 

time: 273 us -> 278 us (1.018)
  waiting for transfers between devices: 35.9 us -> 51.4 us
  blocking collectives: 15.1 us -> 0 us
  starting transfers between devices: 31.4 us -> 37.4 us
  loops' own time: 66.1 us -> 62.1 us
    all_gather x1 -> x0, blocking collectives: 15.1 us -> none  [per_device(): every_rim = lax.all_gather(change_rim, 'ang', axis=0, tiled=True)]
    ppermute x2, waiting for transfers between devices: 1.32 us -> 11.1 us  [padded_2(): lax.ppermute(lax.slice_in_dim(block, block.shape[dim] - width, None, axis...]
    ppermute x0 -> x3, waiting for transfers between devices: none -> 9.28 us  [the longest x2 9.28 us: per_device(): from_left = lax.ppermute(from_left, 'ang', right)]
    ppermute x0 -> x3, starting transfers between devices: none -> 4.25 us  [the longest x1 3.66 us: per_device(): from_right = lax.ppermute(from_right, 'ang', backward_2)]
    ppermute x28, waiting for transfers between devices: 34.5 us -> 30.3 us  [passed_along(): return lax.ppermute(value, axis, pairs)]
    another operation x4, loops' own time: 65.2 us -> 61.5 us  [deposit(): return lax.fori_loop(0, frame_total, add_one, target)]
    dot_general x1 -> x4, matrix products: 3.62 us -> 5.75 us  [the longest x3 4.77 us: per_device(): jnp.einsum('azxk,acky->czxy', lax.dynamic_slice_in_dim(back_pick, (place...]
  transfers between devices with their start and end apart: 32 -> 35, of which waited for: 21 -> 19; matrix products, arithmetic and copies ran while one was open for 18% -> 15% of each run, Pallas kernels for 0% -> 0%
where the time goes in v1:
time: 278 us; the launch traced here: 274 us
  local copies, waits for them, and re-layouts  72.8 us (26%)
  loops' own time  62.1 us (22%)
  waiting for transfers between devices  51.4 us (18%)
  matrix products  44.6 us (16%)
  starting transfers between devices  37.4 us (13%)
  other arithmetic  4.71 us (2%)
    another operation x4, loops' own time, deposit(): return lax.fori_loop(0, frame_total, add_one, target)  61.5 us
    ppermute x28, waiting for transfers between devices, passed_along(): return lax.ppermute(value, axis, pairs)  30.3 us
    ppermute x28, starting transfers between devices, passed_along(): return lax.ppermute(value, axis, pairs)  27.8 us
    dynamic_update_slice x16, local copies, waits for them, and re-layouts, add_one(): return lax.dynamic_update_slice(running, current + addition, corner)  25 us
    gather x36, local copies, waits for them, and re-layouts  24 us
    dynamic_slice x32, local copies, waits for them, and re-layouts, add_one(): corner = (0,) * leading + (start_cols[frame_index], start_rows[frame_index])  19.6 us
    ppermute x2, waiting for transfers between devices, padded_2(): lax.ppermute(lax.slice_in_dim(block, block.shape[dim] - width, None, axis...  11.1 us
    ppermute x2, waiting for transfers between devices, per_device(): from_left = lax.ppermute(from_left, 'ang', right)  9.28 us
  transfers between devices with their start and end apart: 35, of which 19 were waited for; matrix products, arithmetic and copies ran while one was open for 15% of the time, Pallas kernels for 0%

profile of v1, /device:TPU:0, one launch (start us, length us, event | category | flops | bytes accessed | tf_op | source)
XLA Modules:
  0.0 274.0 jit_solution(14299085803101776814)
XLA Ops:
  1.9 26.2 %while.56 = (s32[]{:T(128)}, f32[160,256]{1,0:T(8,128)S(1)}, s32[4]{0:T(128)S(1)}, s32[4]{0:T(128)S(1)}, f32[128,128]{1,0:T(8,128)S(1)}, /*index=5*/s32[]{:T(128)}, s32[]{:T(128)}, s32[]{:T(128)}, s32[]{:T(128)}) while((s32[]{:T(128)}, f32[160,256]{1,0:T(8,128)S(1)}, s32[4]{0:T(128)S(1)}, s32[4]{0:T(128)S(1)}, f32[128,128]{1,0:T(8,128)S(1)}, ...), condition=%wide.region_3.4_spmd, body=%wide.region_2.3_spmd.sunk | while | flops 16392 | bytes 327885 | solution.py:71
  19.6 1.7 dynamic_update_slice.33
  26.4 1.7 dynamic_update_slice.33
  28.8 4.0 %collective-permute-start.10 = (f32[32,256]{1,0:T(8,128)}, f32[32,256]{1,0:T(8,128)S(1)}, u32[]{:S(2)}, u32[]{:S(2)}) collective-permute-start(f32[32,256]{1,0:T(8,128)} %get-tuple-element.535), channel_id=1, source_target_pairs={{0,24},{4,28},{8,0},{12,4},{16,8},{20,12},{24,16},{28,20},{1,25},{... | collective-permute-start | bytes 98312 | tf_op jit(solution)/shard_map/ppermute | solution.py:34
  32.8 2.1 fusion.393
  34.9 2.1 collective-permute-start
  37.8 10.5 %collective-permute-done = f32[2,32,8,256]{3,2,1,0:T(8,128)} collective-permute-done((f32[2,32,8,256]{3,2,1,0:T(8,128)}, f32[2,32,8,256]{3,2,1,0:T(8,128)}, u32[]{:S(2)}, u32[]{:S(2)}) %collective-permute-start) | collective-permute-done | bytes 524320 | tf_op jit(solution)/shard_map/ppermute | solution.py:23
  48.9 2.5 fusion.30
  51.4 1.6 collective-permute-start.2
  53.1 4.2 %collective-permute-done.2 = f32[1,2,32,256]{3,2,1,0:T(8,128)S(1)} collective-permute-done((f32[1,2,32,256]{3,2,1,0:T(8,128)S(1)}, f32[1,2,32,256]{3,2,1,0:T(8,128)S(1)}, u32[]{:S(2)}, u32[]{:S(2)}) %collective-permute-start.2) | collective-permute-done | bytes 65568 | tf_op jit(solution)/shard_map/ppermute | solution.py:34
  57.4 4.5 %collective-permute-done.3 = f32[1,2,32,256]{3,2,1,0:T(8,128)S(1)} collective-permute-done((f32[1,2,32,256]{3,2,1,0:T(8,128)S(1)}, f32[1,2,32,256]{3,2,1,0:T(8,128)S(1)}, u32[]{:S(2)}, u32[]{:S(2)}) %collective-permute-start.3) | collective-permute-done | bytes 65568 | tf_op jit(solution)/shard_map/ppermute | solution.py:34
  61.9 1.9 collective-permute-done.4
  64.5 4.1 %collective-permute-done.5 = f32[1,2,32,256]{3,2,1,0:T(8,128)S(1)} collective-permute-done((f32[1,2,32,256]{3,2,1,0:T(8,128)S(1)}, f32[1,2,32,256]{3,2,1,0:T(8,128)S(1)}, u32[]{:S(2)}, u32[]{:S(2)}) %collective-permute-start.5) | collective-permute-done | bytes 65568 | tf_op jit(solution)/shard_map/ppermute | solution.py:34
  68.6 8.4 %while.59 = (s32[]{:T(128)}, f32[1,2,160,256]{3,2,1,0:T(8,128)S(1)}, s32[4,4]{1,0:T(4,128)S(1)}, f32[4,1,2,128,128]{4,3,0,2,1:T(8,128)S(1)}, s32[]{:T(128)}) while((s32[]{:T(128)}, f32[1,2,160,256]{3,2,1,0:T(8,128)S(1)}, s32[4,4]{1,0:T(4,128)S(1)}, f32[4,1,2,128,128]{4,3,0,2,1:T(8,128)S(1)}, s32[]{:T(128)}) %tuple.169), condition=%wide.while_cond, body=%wide.while_body.sunk | while | flops 2 | bytes 262277 | solution.py:78
  69.3 1.4 bitcast_dynamic-update-slice_fusion.6
  73.4 1.4 bitcast_dynamic-update-slice_fusion.6
  75.5 1.4 bitcast_dynamic-update-slice_fusion.6
  89.5 27.2 %while.55 = (s32[]{:T(128)}, f32[1,2,160,256]{3,2,1,0:T(8,128)S(1)}, s32[4]{0:T(128)S(1)}, s32[4]{0:T(128)S(1)}, f32[1,2,4,128,128]{4,3,2,1,0:T(8,128)S(1)}, /*index=5*/s32[]{:T(128)}, s32[]{:T(128)}, s32[]{:T(128)}, s32[]{:T(128)}) while((s32[]{:T(128)}, f32[1,2,160,256]{3,2,1,0:T(8,128)S(1)}, s32[4]{0:T(128)S(1)}, s32[4]{0:T(128)S(1)}, ...), condition=%wide.region_1.2_spmd, body=%wide.region_0.1_spmd.sunk | while | flops 32776 | bytes 655569 | solution.py:71
  107.3 2.1 dynamic_update_slice.32
  114.6 2.1 dynamic_update_slice.32
  118.9 2.6 collective-permute-start.7
  122.3 1.5 collective-permute-done.9
  125.1 2.3 collective-permute-start.17
  127.9 2.4 collective-permute-done.14
  130.3 2.1 collective-permute-done.15
  132.5 8.0 %while.60 = (s32[]{:T(128)}, f32[1,2,160,256]{3,2,1,0:T(8,128)S(1)}, s32[4,4]{1,0:T(4,128)S(1)}, f32[4,1,2,128,128]{4,3,0,2,1:T(8,128)S(1)}, s32[]{:T(128)}) while((s32[]{:T(128)}, f32[1,2,160,256]{3,2,1,0:T(8,128)S(1)}, s32[4,4]{1,0:T(4,128)S(1)}, f32[4,1,2,128,128]{4,3,0,2,1:T(8,128)S(1)}, s32[]{:T(128)}) %tuple.190), condition=%wide.while_cond.1, body=%wide.while_body.1.sunk | while | flops 2 | bytes 262277 | solution.py:78
  152.7 27.2 %while.57 = (s32[]{:T(128)}, f32[1,2,160,256]{3,2,1,0:T(8,128)S(1)}, s32[4]{0:T(128)S(1)}, s32[4]{0:T(128)S(1)}, f32[1,2,4,128,128]{4,3,2,1,0:T(8,128)S(1)}, /*index=5*/s32[]{:T(128)}, s32[]{:T(128)}, s32[]{:T(128)}, s32[]{:T(128)}) while((s32[]{:T(128)}, f32[1,2,160,256]{3,2,1,0:T(8,128)S(1)}, s32[4]{0:T(128)S(1)}, s32[4]{0:T(128)S(1)}, ...), condition=%wide.region_5.6_spmd, body=%wide.region_4.5_spmd.sunk | while | flops 32776 | bytes 655569 | solution.py:71
  170.5 2.1 dynamic_update_slice.34
  177.8 2.1 dynamic_update_slice.34
  182.1 2.6 collective-permute-start.19
  184.7 2.1 collective-permute-done.21
  187.5 2.7 collective-permute-start.25
  190.9 1.8 collective-permute-done.22
  192.7 2.7 collective-permute-done.23
  195.6 8.2 %while.61 = (s32[]{:T(128)}, f32[1,2,160,256]{3,2,1,0:T(8,128)S(1)}, s32[4,4]{1,0:T(4,128)S(1)}, f32[4,1,2,128,128]{4,3,0,2,1:T(8,128)S(1)}, s32[]{:T(128)}) while((s32[]{:T(128)}, f32[1,2,160,256]{3,2,1,0:T(8,128)S(1)}, s32[4,4]{1,0:T(4,128)S(1)}, f32[4,1,2,128,128]{4,3,0,2,1:T(8,128)S(1)}, s32[]{:T(128)}) %tuple.191), condition=%wide.while_cond.2, body=%wide.while_body.2.sunk | while | flops 2 | bytes 262277 | solution.py:78
  198.3 1.4 bitcast_dynamic-update-slice_fusion.8
  200.4 1.4 bitcast_dynamic-update-slice_fusion.8
  202.4 1.4 bitcast_dynamic-update-slice_fusion.8
  216.1 27.2 %while.58 = (s32[]{:T(128)}, f32[1,2,160,256]{3,2,1,0:T(8,128)S(1)}, s32[4]{0:T(128)S(1)}, s32[4]{0:T(128)S(1)}, f32[1,2,4,128,128]{4,3,2,1,0:T(8,128)S(1)}, /*index=5*/s32[]{:T(128)}, s32[]{:T(128)}, s32[]{:T(128)}, s32[]{:T(128)}) while((s32[]{:T(128)}, f32[1,2,160,256]{3,2,1,0:T(8,128)S(1)}, s32[4]{0:T(128)S(1)}, s32[4]{0:T(128)S(1)}, ...), condition=%wide.region_7.8_spmd, body=%wide.region_6.7_spmd.sunk | while | flops 32776 | bytes 655569 | solution.py:71
  233.9 2.1 dynamic_update_slice.35
  241.2 2.1 dynamic_update_slice.35
  245.5 2.6 collective-permute-start.27
  248.2 1.6 collective-permute-done.29
  250.7 2.3 collective-permute-start.31
  254.5 3.7 %collective-permute-start.32 = (f32[1,2,48,256]{3,2,1,0:T(8,128)S(1)}, f32[1,2,48,256]{3,2,1,0:T(8,128)S(1)}, u32[]{:S(2)}, u32[]{:S(2)}) collective-permute-start(f32[1,2,48,256]{3,2,1,0:T(8,128)S(1)} %pad_maximum_fusion.3), channel_id=1, source_target_pairs={{0,3},{1,0},{2,1},{3,2},{4,7},{5,4},{6,5},{7,6},{8,11},{9,8},{10,9... | collective-permute-start | bytes 294920 | tf_op jit(solution)/shard_map/ppermute | solution.py:186
  259.1 5.4 %collective-permute-done.33 = f32[1,2,48,256]{3,2,1,0:T(8,128)S(1)} collective-permute-done((f32[1,2,48,256]{3,2,1,0:T(8,128)S(1)}, f32[1,2,48,256]{3,2,1,0:T(8,128)S(1)}, u32[]{:S(2)}, u32[]{:S(2)}) %collective-permute-start.33) | collective-permute-done | bytes 98336 | tf_op jit(solution)/shard_map/ppermute | solution.py:184
  267.1 3.8 %collective-permute-done.34 = f32[1,2,48,256]{3,2,1,0:T(8,128)S(1)} collective-permute-done((f32[1,2,48,256]{3,2,1,0:T(8,128)S(1)}, f32[1,2,48,256]{3,2,1,0:T(8,128)S(1)}, u32[]{:S(2)}, u32[]{:S(2)}) %collective-permute-start.34) | collective-permute-done | bytes 98336 | tf_op jit(solution)/shard_map/ppermute | solution.py:184
  271.0 2.8 %bitcast_add_fusion.3 = f32[2,32,32,256]{3,2,1,0:T(8,128)} fusion(f32[2,32,32,256]{3,2,1,0:T(8,128)S(1)} %copy-done, f32[2,256,32,32]{1,3,2,0:T(8,128)S(1)} %fusion.36, f32[2,256,32,32]{1,3,2,0:T(8,128)S(1)} %fusion.40, f32[2,256,32,32]{1,3,2,0:T(8,128)S(1)} %fusion.38, pred[4,32,32,48]{3,2,1,0:T(32,128)(4,1)S(1)} %iota_compare_fusion, s32[]{:T(128)S(6)} %select_n.251, ...), kind=kOutput, calls=%fused_computation.16 | convolution fusion | flops 304611328 | bytes 10715140 | tf_op jit(solution)/shard_map/azxk,acky->czxy/dot_general | solution.py:195
  (250 shorter events, 103.8 us)
Async XLA Ops:
  1.9 35.8 %copy-start.2 = (s32[4,32]{1,0:T(4,128)S(1)}, s32[4,32]{1,0:T(4,128)}, u32[]{:S(2)}) copy-start(s32[4,32]{1,0:T(4,128)} %param.17) | copy-start | bytes 1540
  1.9 35.9 %copy-start.1 = (f32[2,128,128]{2,1,0:T(8,128)S(1)}, f32[2,128,128]{2,1,0:T(8,128)}, u32[]{:S(2)}) copy-start(f32[2,128,128]{2,1,0:T(8,128)} %param.14) | copy-start | bytes 393220
  1.9 46.9 %copy-start = (f32[2,32,32,256]{3,2,1,0:T(8,128)S(1)}, f32[2,32,32,256]{3,2,1,0:T(8,128)}, u32[]{:S(2)}) copy-start(f32[2,32,32,256]{3,2,1,0:T(8,128)} %param.13) | copy-start | bytes 6291460
  28.8 89.2 %collective-permute-start.10 = (f32[32,256]{1,0:T(8,128)}, f32[32,256]{1,0:T(8,128)S(1)}, u32[]{:S(2)}, u32[]{:S(2)}) collective-permute-start(f32[32,256]{1,0:T(8,128)} %get-tuple-element.535), channel_id=1, source_target_pairs={{0,24},{4,28},{8,0},{12,4},{16,8},{20,12},{24,16},{28,20},{1,25},{... | collective-permute-start | bytes 98312 | tf_op jit(solution)/shard_map/ppermute | solution.py:34
  32.8 86.0 %collective-permute-start.13 = (f32[32,256]{1,0:T(8,128)}, f32[32,256]{1,0:T(8,128)S(1)}, u32[]{:S(2)}, u32[]{:S(2)}) collective-permute-start(f32[32,256]{1,0:T(8,128)} %get-tuple-element.536), channel_id=1, source_target_pairs={{0,8},{4,12},{8,16},{12,20},{16,24},{20,28},{24,0},{28,4},{1,9},{5... | collective-permute-start | bytes 98312 | tf_op jit(solution)/shard_map/ppermute | solution.py:34
  32.8 86.0 %collective-permute-start.12 = (f32[32,256]{1,0:T(8,128)}, f32[32,256]{1,0:T(8,128)}, u32[]{:S(2)}, u32[]{:S(2)}) collective-permute-start(f32[32,256]{1,0:T(8,128)} %get-tuple-element.537), channel_id=1, source_target_pairs={{0,4},{4,8},{8,12},{12,16},{16,20},{20,24},{24,28},{28,0},{1,5},{5... | collective-permute-start | bytes 98312 | tf_op jit(solution)/shard_map/ppermute | solution.py:34
  34.9 13.3 %collective-permute-start = (f32[2,32,8,256]{3,2,1,0:T(8,128)}, f32[2,32,8,256]{3,2,1,0:T(8,128)}, u32[]{:S(2)}, u32[]{:S(2)}) collective-permute-start(f32[2,32,8,256]{3,2,1,0:T(8,128)} %get-tuple-element.509), channel_id=1, source_target_pairs={{0,4},{4,8},{8,12},{12,16},{16,20},{20,24},{24,28},{28,0},{1,5},{5... | collective-permute-start | bytes 1572872 | tf_op jit(solution)/shard_map/ppermute | solution.py:23
  37.0 11.8 %collective-permute-start.1 = (f32[2,32,8,256]{3,2,1,0:T(8,128)S(1)}, f32[2,32,8,256]{3,2,1,0:T(8,128)}, u32[]{:S(2)}, u32[]{:S(2)}) collective-permute-start(f32[2,32,8,256]{3,2,1,0:T(8,128)S(1)} %get-tuple-element.510), channel_id=1, source_target_pairs={{4,0},{8,4},{12,8},{16,12},{20,16},{24,20},{28,24},{0,28},{5,1},{9... | collective-permute-start | bytes 1572872 | tf_op jit(solution)/shard_map/ppermute | solution.py:26
  48.3 73.3 %collective-permute-start.11 = (f32[32,256]{1,0:T(8,128)}, f32[32,256]{1,0:T(8,128)}, u32[]{:S(2)}, u32[]{:S(2)}) collective-permute-start(f32[32,256]{1,0:T(8,128)} %get-tuple-element.538), channel_id=1, source_target_pairs={{0,28},{4,0},{8,4},{12,8},{16,12},{20,16},{24,20},{28,24},{1,29},{... | collective-permute-start | bytes 98312 | tf_op jit(solution)/shard_map/ppermute | solution.py:34
  51.4 5.9 %collective-permute-start.2 = (f32[1,2,32,256]{3,2,1,0:T(8,128)S(1)}, f32[1,2,32,256]{3,2,1,0:T(8,128)S(1)}, u32[]{:S(2)}, u32[]{:S(2)}) collective-permute-start(f32[1,2,32,256]{3,2,1,0:T(8,128)S(1)} %fusion.30), channel_id=1, source_target_pairs={{0,8},{4,12},{8,16},{12,20},{16,24},{20,28},{24,0},{28,4},{1,9},{5... | collective-permute-start | bytes 196616 | tf_op jit(solution)/shard_map/ppermute | solution.py:34
  57.3 4.6 %collective-permute-start.3 = (f32[1,2,32,256]{3,2,1,0:T(8,128)S(1)}, f32[1,2,32,256]{3,2,1,0:T(8,128)S(1)}, u32[]{:S(2)}, u32[]{:S(2)}) collective-permute-start(f32[1,2,32,256]{3,2,1,0:T(8,128)S(1)} %fusion.30), channel_id=1, source_target_pairs={{0,4},{4,8},{8,12},{12,16},{16,20},{20,24},{24,28},{28,0},{1,5},{5... | collective-permute-start | bytes 196616 | tf_op jit(solution)/shard_map/ppermute | solution.py:34
  61.9 1.9 collective-permute-start.4
  63.8 4.8 %collective-permute-start.5 = (f32[1,2,32,256]{3,2,1,0:T(8,128)S(1)}, f32[1,2,32,256]{3,2,1,0:T(8,128)S(1)}, u32[]{:S(2)}, u32[]{:S(2)}) collective-permute-start(f32[1,2,32,256]{3,2,1,0:T(8,128)S(1)} %fusion.30), channel_id=1, source_target_pairs={{0,24},{4,28},{8,0},{12,4},{16,8},{20,12},{24,16},{28,20},{1,25},{... | collective-permute-start | bytes 196616 | tf_op jit(solution)/shard_map/ppermute | solution.py:34
  77.8 4.5 %copy-start.3 = (f32[1,4,128,128]{3,2,1,0:T(8,128)S(1)}, f32[1,4,128,128]{3,2,1,0:T(8,128)}, u32[]{:S(2)}) copy-start(f32[1,4,128,128]{3,2,1,0:T(8,128)} %param.15) | copy-start | bytes 786436
  116.8 4.8 %copy-start.6 = (s32[4]{0:T(128)}, s32[4]{0:T(128)S(1)}, u32[]{:S(2)}) copy-start(s32[4]{0:T(128)S(1)} %get-tuple-element.979) | copy-start | bytes 52
  116.8 5.5 %collective-permute-start.6 = (f32[1,2,32,256]{3,2,1,0:T(8,128)S(1)}, f32[1,2,32,256]{3,2,1,0:T(8,128)S(1)}, u32[]{:S(2)}, u32[]{:S(2)}) collective-permute-start(f32[1,2,32,256]{3,2,1,0:T(8,128)S(1)} %get-tuple-element.531), channel_id=1, source_target_pairs={{0,24},{4,28},{8,0},{12,4},{16,8},{20,12},{24,16},{28,20},{1,25},{... | collective-permute-start | bytes 196616 | tf_op jit(solution)/shard_map/ppermute | solution.py:34
  118.0 5.9 %collective-permute-start.9 = (f32[1,2,32,256]{3,2,1,0:T(8,128)S(1)}, f32[1,2,32,256]{3,2,1,0:T(8,128)S(1)}, u32[]{:S(2)}, u32[]{:S(2)}) collective-permute-start(f32[1,2,32,256]{3,2,1,0:T(8,128)S(1)} %get-tuple-element.532), channel_id=1, source_target_pairs={{0,8},{4,12},{8,16},{12,20},{16,24},{20,28},{24,0},{28,4},{1,9},{5... | collective-permute-start | bytes 196616 | tf_op jit(solution)/shard_map/ppermute | solution.py:34
  118.9 5.5 %collective-permute-start.8 = (f32[1,2,32,256]{3,2,1,0:T(8,128)S(1)}, f32[1,2,32,256]{3,2,1,0:T(8,128)S(1)}, u32[]{:S(2)}, u32[]{:S(2)}) collective-permute-start(f32[1,2,32,256]{3,2,1,0:T(8,128)S(1)} %get-tuple-element.533), channel_id=1, source_target_pairs={{0,4},{4,8},{8,12},{12,16},{16,20},{20,24},{24,28},{28,0},{1,5},{5... | collective-permute-start | bytes 196616 | tf_op jit(solution)/shard_map/ppermute | solution.py:34
  118.9 5.5 %collective-permute-start.7 = (f32[1,2,32,256]{3,2,1,0:T(8,128)S(1)}, f32[1,2,32,256]{3,2,1,0:T(8,128)S(1)}, u32[]{:S(2)}, u32[]{:S(2)}) collective-permute-start(f32[1,2,32,256]{3,2,1,0:T(8,128)S(1)} %get-tuple-element.534), channel_id=1, source_target_pairs={{0,28},{4,0},{8,4},{12,8},{16,12},{20,16},{24,20},{28,24},{1,29},{... | collective-permute-start | bytes 196616 | tf_op jit(solution)/shard_map/ppermute | solution.py:34
  124.5 5.9 %collective-permute-start.14 = (f32[1,2,32,256]{3,2,1,0:T(8,128)S(1)}, f32[1,2,32,256]{3,2,1,0:T(8,128)S(1)}, u32[]{:S(2)}, u32[]{:S(2)}) collective-permute-start(f32[1,2,32,256]{3,2,1,0:T(8,128)S(1)} %add_divide_fusion.1), channel_id=1, source_target_pairs={{0,8},{4,12},{8,16},{12,20},{16,24},{20,28},{24,0},{28,4},{1,9},{5... | collective-permute-start | bytes 196616 | tf_op jit(solution)/shard_map/ppermute | solution.py:34
  125.1 7.3 %collective-permute-start.17 = (f32[1,2,32,256]{3,2,1,0:T(8,128)S(1)}, f32[1,2,32,256]{3,2,1,0:T(8,128)S(1)}, u32[]{:S(2)}, u32[]{:S(2)}) collective-permute-start(f32[1,2,32,256]{3,2,1,0:T(8,128)S(1)} %add_divide_fusion.1), channel_id=1, source_target_pairs={{0,24},{4,28},{8,0},{12,4},{16,8},{20,12},{24,16},{28,20},{1,25},{... | collective-permute-start | bytes 196616 | tf_op jit(solution)/shard_map/ppermute | solution.py:34
  127.4 5.0 %collective-permute-start.16 = (f32[1,2,32,256]{3,2,1,0:T(8,128)S(1)}, f32[1,2,32,256]{3,2,1,0:T(8,128)S(1)}, u32[]{:S(2)}, u32[]{:S(2)}) collective-permute-start(f32[1,2,32,256]{3,2,1,0:T(8,128)S(1)} %add_divide_fusion.1), channel_id=1, source_target_pairs={{0,28},{4,0},{8,4},{12,8},{16,12},{20,16},{24,20},{28,24},{1,29},{... | collective-permute-start | bytes 196616 | tf_op jit(solution)/shard_map/ppermute | solution.py:34
  127.7 4.8 %collective-permute-start.15 = (f32[1,2,32,256]{3,2,1,0:T(8,128)S(1)}, f32[1,2,32,256]{3,2,1,0:T(8,128)S(1)}, u32[]{:S(2)}, u32[]{:S(2)}) collective-permute-start(f32[1,2,32,256]{3,2,1,0:T(8,128)S(1)} %add_divide_fusion.1), channel_id=1, source_target_pairs={{0,4},{4,8},{8,12},{12,16},{16,20},{20,24},{24,28},{28,0},{1,5},{5... | collective-permute-start | bytes 196616 | tf_op jit(solution)/shard_map/ppermute | solution.py:34
  141.3 4.5 %copy-start.4 = (f32[1,4,128,128]{3,2,1,0:T(8,128)S(1)}, f32[1,4,128,128]{3,2,1,0:T(8,128)}, u32[]{:S(2)}) copy-start(f32[1,4,128,128]{3,2,1,0:T(8,128)} %param.15) | copy-start | bytes 786436
  150.3 2.5 copy-start.7
  180.0 4.7 %collective-permute-start.18 = (f32[1,2,32,256]{3,2,1,0:T(8,128)S(1)}, f32[1,2,32,256]{3,2,1,0:T(8,128)S(1)}, u32[]{:S(2)}, u32[]{:S(2)}) collective-permute-start(f32[1,2,32,256]{3,2,1,0:T(8,128)S(1)} %get-tuple-element.527), channel_id=1, source_target_pairs={{0,24},{4,28},{8,0},{12,4},{16,8},{20,12},{24,16},{28,20},{1,25},{... | collective-permute-start | bytes 196616 | tf_op jit(solution)/shard_map/ppermute | solution.py:34
  181.3 5.6 %collective-permute-start.21 = (f32[1,2,32,256]{3,2,1,0:T(8,128)S(1)}, f32[1,2,32,256]{3,2,1,0:T(8,128)S(1)}, u32[]{:S(2)}, u32[]{:S(2)}) collective-permute-start(f32[1,2,32,256]{3,2,1,0:T(8,128)S(1)} %get-tuple-element.528), channel_id=1, source_target_pairs={{0,8},{4,12},{8,16},{12,20},{16,24},{20,28},{24,0},{28,4},{1,9},{5... | collective-permute-start | bytes 196616 | tf_op jit(solution)/shard_map/ppermute | solution.py:34
  182.1 5.0 %collective-permute-start.20 = (f32[1,2,32,256]{3,2,1,0:T(8,128)S(1)}, f32[1,2,32,256]{3,2,1,0:T(8,128)S(1)}, u32[]{:S(2)}, u32[]{:S(2)}) collective-permute-start(f32[1,2,32,256]{3,2,1,0:T(8,128)S(1)} %get-tuple-element.529), channel_id=1, source_target_pairs={{0,4},{4,8},{8,12},{12,16},{16,20},{20,24},{24,28},{28,0},{1,5},{5... | collective-permute-start | bytes 196616 | tf_op jit(solution)/shard_map/ppermute | solution.py:34
  182.1 5.0 %collective-permute-start.19 = (f32[1,2,32,256]{3,2,1,0:T(8,128)S(1)}, f32[1,2,32,256]{3,2,1,0:T(8,128)S(1)}, u32[]{:S(2)}, u32[]{:S(2)}) collective-permute-start(f32[1,2,32,256]{3,2,1,0:T(8,128)S(1)} %get-tuple-element.530), channel_id=1, source_target_pairs={{0,28},{4,0},{8,4},{12,8},{16,12},{20,16},{24,20},{28,24},{1,29},{... | collective-permute-start | bytes 196616 | tf_op jit(solution)/shard_map/ppermute | solution.py:34
  187.2 5.6 %collective-permute-start.22 = (f32[1,2,32,256]{3,2,1,0:T(8,128)S(1)}, f32[1,2,32,256]{3,2,1,0:T(8,128)S(1)}, u32[]{:S(2)}, u32[]{:S(2)}) collective-permute-start(f32[1,2,32,256]{3,2,1,0:T(8,128)S(1)} %add_divide_fusion), channel_id=1, source_target_pairs={{0,8},{4,12},{8,16},{12,20},{16,24},{20,28},{24,0},{28,4},{1,9},{5... | collective-permute-start | bytes 196616 | tf_op jit(solution)/shard_map/ppermute | solution.py:34
  187.5 8.0 %collective-permute-start.25 = (f32[1,2,32,256]{3,2,1,0:T(8,128)S(1)}, f32[1,2,32,256]{3,2,1,0:T(8,128)S(1)}, u32[]{:S(2)}, u32[]{:S(2)}) collective-permute-start(f32[1,2,32,256]{3,2,1,0:T(8,128)S(1)} %add_divide_fusion), channel_id=1, source_target_pairs={{0,24},{4,28},{8,0},{12,4},{16,8},{20,12},{24,16},{28,20},{1,25},{... | collective-permute-start | bytes 196616 | tf_op jit(solution)/shard_map/ppermute | solution.py:34
  190.1 5.4 %collective-permute-start.24 = (f32[1,2,32,256]{3,2,1,0:T(8,128)S(1)}, f32[1,2,32,256]{3,2,1,0:T(8,128)S(1)}, u32[]{:S(2)}, u32[]{:S(2)}) collective-permute-start(f32[1,2,32,256]{3,2,1,0:T(8,128)S(1)} %add_divide_fusion), channel_id=1, source_target_pairs={{0,28},{4,0},{8,4},{12,8},{16,12},{20,16},{24,20},{28,24},{1,29},{... | collective-permute-start | bytes 196616 | tf_op jit(solution)/shard_map/ppermute | solution.py:34
  190.9 4.6 %collective-permute-start.23 = (f32[1,2,32,256]{3,2,1,0:T(8,128)S(1)}, f32[1,2,32,256]{3,2,1,0:T(8,128)S(1)}, u32[]{:S(2)}, u32[]{:S(2)}) collective-permute-start(f32[1,2,32,256]{3,2,1,0:T(8,128)S(1)} %add_divide_fusion), channel_id=1, source_target_pairs={{0,4},{4,8},{8,12},{12,16},{16,20},{20,24},{24,28},{28,0},{1,5},{5... | collective-permute-start | bytes 196616 | tf_op jit(solution)/shard_map/ppermute | solution.py:34
  204.6 4.5 %copy-start.5 = (f32[1,4,128,128]{3,2,1,0:T(8,128)S(1)}, f32[1,4,128,128]{3,2,1,0:T(8,128)}, u32[]{:S(2)}) copy-start(f32[1,4,128,128]{3,2,1,0:T(8,128)} %param.15) | copy-start | bytes 786436
  243.4 4.8 %collective-permute-start.26 = (f32[1,2,32,256]{3,2,1,0:T(8,128)S(1)}, f32[1,2,32,256]{3,2,1,0:T(8,128)S(1)}, u32[]{:S(2)}, u32[]{:S(2)}) collective-permute-start(f32[1,2,32,256]{3,2,1,0:T(8,128)S(1)} %get-tuple-element.523), channel_id=1, source_target_pairs={{0,24},{4,28},{8,0},{12,4},{16,8},{20,12},{24,16},{28,20},{1,25},{... | collective-permute-start | bytes 196616 | tf_op jit(solution)/shard_map/ppermute | solution.py:34
  244.4 5.4 %collective-permute-start.29 = (f32[1,2,32,256]{3,2,1,0:T(8,128)S(1)}, f32[1,2,32,256]{3,2,1,0:T(8,128)S(1)}, u32[]{:S(2)}, u32[]{:S(2)}) collective-permute-start(f32[1,2,32,256]{3,2,1,0:T(8,128)S(1)} %get-tuple-element.524), channel_id=1, source_target_pairs={{0,8},{4,12},{8,16},{12,20},{16,24},{20,28},{24,0},{28,4},{1,9},{5... | collective-permute-start | bytes 196616 | tf_op jit(solution)/shard_map/ppermute | solution.py:34
  245.4 4.8 %collective-permute-start.28 = (f32[1,2,32,256]{3,2,1,0:T(8,128)S(1)}, f32[1,2,32,256]{3,2,1,0:T(8,128)S(1)}, u32[]{:S(2)}, u32[]{:S(2)}) collective-permute-start(f32[1,2,32,256]{3,2,1,0:T(8,128)S(1)} %get-tuple-element.525), channel_id=1, source_target_pairs={{0,4},{4,8},{8,12},{12,16},{16,20},{20,24},{24,28},{28,0},{1,5},{5... | collective-permute-start | bytes 196616 | tf_op jit(solution)/shard_map/ppermute | solution.py:34
  245.5 4.8 %collective-permute-start.27 = (f32[1,2,32,256]{3,2,1,0:T(8,128)S(1)}, f32[1,2,32,256]{3,2,1,0:T(8,128)S(1)}, u32[]{:S(2)}, u32[]{:S(2)}) collective-permute-start(f32[1,2,32,256]{3,2,1,0:T(8,128)S(1)} %get-tuple-element.526), channel_id=1, source_target_pairs={{0,28},{4,0},{8,4},{12,8},{16,12},{20,16},{24,20},{28,24},{1,29},{... | collective-permute-start | bytes 196616 | tf_op jit(solution)/shard_map/ppermute | solution.py:34
  250.3 4.1 %collective-permute-start.30 = (f32[1,2,8,256]{3,2,1,0:T(8,128)S(1)}, f32[1,2,8,256]{3,2,1,0:T(8,128)S(1)}, u32[]{:S(2)}, u32[]{:S(2)}) collective-permute-start(f32[1,2,8,256]{3,2,1,0:T(8,128)S(1)} %get-tuple-element.541), channel_id=1, source_target_pairs={{0,4},{4,8},{8,12},{12,16},{16,20},{20,24},{24,28},{28,0},{1,5},{5... | collective-permute-start | bytes 49160 | tf_op jit(solution)/shard_map/ppermute | solution.py:23
  250.7 3.7 %collective-permute-start.31 = (f32[1,2,8,256]{3,2,1,0:T(8,128)S(1)}, f32[1,2,8,256]{3,2,1,0:T(8,128)S(1)}, u32[]{:S(2)}, u32[]{:S(2)}) collective-permute-start(f32[1,2,8,256]{3,2,1,0:T(8,128)S(1)} %get-tuple-element.542), channel_id=1, source_target_pairs={{4,0},{8,4},{12,8},{16,12},{20,16},{24,20},{28,24},{0,28},{5,1},{9... | collective-permute-start | bytes 49160 | tf_op jit(solution)/shard_map/ppermute | solution.py:26
  254.5 11.7 %collective-permute-start.32 = (f32[1,2,48,256]{3,2,1,0:T(8,128)S(1)}, f32[1,2,48,256]{3,2,1,0:T(8,128)S(1)}, u32[]{:S(2)}, u32[]{:S(2)}) collective-permute-start(f32[1,2,48,256]{3,2,1,0:T(8,128)S(1)} %pad_maximum_fusion.3), channel_id=1, source_target_pairs={{0,3},{1,0},{2,1},{3,2},{4,7},{5,4},{6,5},{7,6},{8,11},{9,8},{10,9... | collective-permute-start | bytes 294920 | tf_op jit(solution)/shard_map/ppermute | solution.py:186
  258.2 6.4 %collective-permute-start.33 = (f32[1,2,48,256]{3,2,1,0:T(8,128)S(1)}, f32[1,2,48,256]{3,2,1,0:T(8,128)S(1)}, u32[]{:S(2)}, u32[]{:S(2)}) collective-permute-start(f32[1,2,48,256]{3,2,1,0:T(8,128)S(1)} %pad_maximum_fusion.3), channel_id=1, source_target_pairs={{0,1},{1,2},{2,3},{3,0},{4,5},{5,6},{6,7},{7,4},{8,9},{9,10},{10,1... | collective-permute-start | bytes 294920 | tf_op jit(solution)/shard_map/ppermute | solution.py:184
  264.6 6.4 %collective-permute-start.34 = (f32[1,2,48,256]{3,2,1,0:T(8,128)S(1)}, f32[1,2,48,256]{3,2,1,0:T(8,128)S(1)}, u32[]{:S(2)}, u32[]{:S(2)}) collective-permute-start(f32[1,2,48,256]{3,2,1,0:T(8,128)S(1)} %collective-permute-done.33), channel_id=1, source_target_pairs={{0,1},{1,2},{2,3},{3,0},{4,5},{5,6},{6,7},{7,4},{8,9},{9,10},{10,1... | collective-permute-start | bytes 294920 | tf_op jit(solution)/shard_map/ppermute | solution.py:184
